TPU v7x, 512 devices: a whole 4x4x16 slice. The times are simulated.
512 devices in a mesh: seq: 64 (over z, y_hi, core), mp: 8 (over y_lo, x).
Axes of the slice: x: 4, y: 4 (y_hi: 2, y_lo: 2; y = y_hi * 2 + y_lo), z: 16, core: 2. Of those that a mesh axis runs over, the one named last changes fastest.
Arguments:
- query: bfloat16 [1, 64, 64, 1024], P(None, 'seq', None, 'mp'), may hold values from -6 to 6
- keys: bfloat16 [1, 64, 64, 1024], P(None, 'seq', None, 'mp'), may hold values from -6 to 6
- values: bfloat16 [1, 64, 64, 1024], P(None, 'seq', None, 'mp'), may hold values from -6 to 6
- resid: bfloat16 [1, 64, 64, 1920], P(None, 'seq', 'mp'), may hold values from -4 to 4
- out_weight: bfloat16 [1024, 1920], P('mp'), may hold values from -0.1875 to 0.1875
- norm_gain: float32 [1920], replicated, may hold values from 0.1 to 1.9
- norm_bias: float32 [1920], replicated, may hold values from -3 to 3
- deconv1_weight: bfloat16 [384, 4, 4, 1920], P('mp'), may hold values from -0.0625 to 0.0625
- deconv1_bias: float32 [384], P('mp'), may hold values from -3 to 3
- deconv2_weight: bfloat16 [384, 4, 4, 384], P('mp'), may hold values from -0.15625 to 0.15625
- deconv2_bias: float32 [384], P('mp'), may hold values from -3 to 3
- final_weight: bfloat16 [384, 308], replicated, may hold values from -0.3125 to 0.3125
- final_bias: float32 [308], replicated, may hold values from -3 to 3
Outputs:
- heatmaps: bfloat16 [1, 256, 256, 308], P(None, 'seq', 'mp')
All inputs are finite; a program needn't handle non-finite values.
Results may differ from a plain program's by a relative error of at most 0.012.
Values may be sent and summed in bfloat16 or wider, within the bound.
A program may use at most 64 MiB of HBM per device.

v0:
```python
import jax
import jax.numpy as jnp
from jax import lax
from jax.sharding import PartitionSpec as P

HEAD_DIM = 64


TAP_TABLE = (((1, 1), (0, 3)), ((2, 0), (1, 2)))
EPSILON = 1e-06


def with_halo(array, sides, width):
    for axis, dim in sides:
        size, length = (lax.axis_size(axis), array.shape[dim])
        up = [(i, (i + 1) % size) for i in range(size - 1)]
        down = [(j, i) for i, j in up]
        last = lax.slice_in_dim(array, length - width, length, axis=dim)
        first = lax.slice_in_dim(array, 0, width, axis=dim)
        before = lax.ppermute(last, axis, up)
        after = lax.ppermute(first, axis, down)
        array = jnp.concatenate([before, array, after], axis=dim)
    return array


def tap_product(window, weight, kernel_row, kernel_col):
    tap = weight[:, kernel_row, kernel_col, :]
    return lax.dot_general(
        window, tap, (((3,), (1,)), ((), ())), preferred_element_type=jnp.float32
    )


def half_rows(padded, weight, tap_pairs, first_row, row_count):
    col_count = padded.shape[2] - 2
    halves = []
    for col_parity in range(2):
        summed = None
        for pad_row, kernel_row in tap_pairs:
            for pad_col, kernel_col in TAP_TABLE[col_parity]:
                window = padded[
                    :,
                    first_row + pad_row : first_row + pad_row + row_count,
                    pad_col : pad_col + col_count,
                    :,
                ]
                product = tap_product(window, weight, kernel_row, kernel_col)
                summed = product if summed is None else summed + product
        halves.append(summed)
    stacked = jnp.stack(halves, axis=3)
    return stacked.reshape(stacked.shape[0], row_count, 2 * col_count, stacked.shape[-1])


def upsample(padded, weight, row_count):
    even_rows = half_rows(padded, weight, TAP_TABLE[0], 0, row_count)
    odd_rows = half_rows(padded, weight, TAP_TABLE[1], 0, row_count)
    stacked = jnp.stack([even_rows, odd_rows], axis=2)
    return stacked.reshape(stacked.shape[0], 2 * row_count, stacked.shape[3], stacked.shape[4])


def pad_columns(field):
    return jnp.pad(field, ((0, 0), (0, 0), (1, 1), (0, 0)))


def layer_norm(stream, norm_gain, norm_bias):
    center = jnp.mean(stream, axis=-1, keepdims=True)
    shifted = stream - center
    variance = jnp.mean(shifted * shifted, axis=-1, keepdims=True)
    return (shifted * lax.rsqrt(variance + EPSILON) * norm_gain + norm_bias).astype(jnp.bfloat16)


def local(
    query,
    keys,
    values,
    resid,
    out_weight,
    norm_gain,
    norm_bias,
    deconv1_weight,
    deconv1_bias,
    deconv2_weight,
    deconv2_bias,
    final_weight,
    final_bias,
):
    frame_count, row_count, col_count, feature_width = query.shape
    local_heads = feature_width // HEAD_DIM
    score_scale = HEAD_DIM ** (-0.5)
    query_count = row_count * col_count
    queries = query.reshape(frame_count, query_count, local_heads, HEAD_DIM)
    start_max = jnp.full((frame_count, query_count, local_heads), -1e30, jnp.float32)
    running_max = start_max
    key_piece = lax.all_gather(keys, "seq", axis=1, tiled=True).reshape(
        frame_count, -1, local_heads, HEAD_DIM
    )
    value_piece = lax.all_gather(values, "seq", axis=1, tiled=True).reshape(
        frame_count, -1, local_heads, HEAD_DIM
    )
    scores = (
        jnp.einsum("fqhd,fkhd->fqhk", queries, key_piece, preferred_element_type=jnp.float32)
        * score_scale
    )
    fresh_max = jnp.maximum(running_max, jnp.max(scores, axis=-1))
    exps = jnp.exp(scores - fresh_max[..., None])
    denominator = jnp.sum(exps, axis=-1)
    weighted = jnp.einsum(
        "fqhk,fkhd->fqhd",
        exps.astype(jnp.bfloat16),
        value_piece,
        preferred_element_type=jnp.float32,
    )
    running_max, denominator, weighted = (fresh_max, denominator, weighted)
    attended = (
        (weighted / denominator[..., None])
        .astype(jnp.bfloat16)
        .reshape(frame_count, row_count, col_count, feature_width)
    )
    partial_value = jnp.dot(attended, out_weight, preferred_element_type=jnp.float32)
    summed = lax.psum(partial_value.astype(jnp.bfloat16), "mp").astype(jnp.float32)
    full_resid = lax.all_gather(resid, "mp", axis=2, tiled=True)
    normed = layer_norm(full_resid.astype(jnp.float32) + summed, norm_gain, norm_bias)
    rimmed = with_halo(normed, (("seq", 1),), 1)
    padded = pad_columns(rimmed)
    deconv_one = upsample(padded, deconv1_weight, row_count)
    hidden_one = jnp.maximum(deconv_one + deconv1_bias, 0.0).astype(jnp.bfloat16)
    gathered = lax.all_gather(hidden_one, "mp", axis=3, tiled=True)
    middle = with_halo(gathered, (("seq", 1),), 1)
    deconv_two = upsample(pad_columns(middle), deconv2_weight, 2 * row_count)
    hidden_two = jnp.maximum(deconv_two + deconv2_bias, 0.0).astype(jnp.bfloat16)
    return (
        jnp.dot(
            lax.all_to_all(hidden_two, "mp", split_axis=2, concat_axis=3, tiled=True),
            final_weight,
            preferred_element_type=jnp.float32,
        )
        + final_bias
    ).astype(jnp.bfloat16)


def solution(mesh):
    placed = (
        P(None, "seq", None, "mp"),
        P(None, "seq", None, "mp"),
        P(None, "seq", None, "mp"),
        P(None, "seq", "mp", None),
        P("mp", None),
        P(),
        P(),
        P("mp", None, None, None),
        P("mp"),
        P("mp", None, None, None),
        P("mp"),
        P(),
        P(),
    )
    return jax.shard_map(
        local, mesh=mesh, in_specs=placed, out_specs=P(None, "seq", "mp", None), check_vma=False
    )
```

profile of v0, /device:TPU:113, one launch (start us, length us, event | category | flops | bytes accessed | tf_op | source)
XLA Modules:
  0.0 476.3 jit_solution(8627854209364443066)
XLA Ops:
  6.5 0.7 all-gather.3.cloned.1.call-update
  7.3 0.7 all-gather.5.cloned.1.call-update
  8.1 0.8 reshape.266
  8.9 22.4 %all_gather.12 = bf16[1,1,64,1920]{3,2,1,0:T(8,128)(2,1)S(1)} all-gather(bf16[1,1,8,1920]{3,2,1,0:T(8,128)(2,1)} %param.16), channel_id=1, replica_groups=mesh['seq'=64,'mp'=8] {'mp'}, dimensions={2}, use_global_device_ids=true | all-gather | bytes 276480 | tf_op jit(solution)/shard_map/all_gather | solution.py:120
  31.2 10.4 %fusion.86 = (bf16[48,1,1,1920]{3,2,1,0:T(2,128)(2,1)}, bf16[48,1,1,1920]{3,2,1,0:T(2,128)(2,1)}, bf16[48,1,1,1920]{3,2,1,0:T(2,128)(2,1)}, bf16[48,1,1,1920]{3,...) fusion(bf16[48,4,4,1920]{3,2,1,0:T(4,128)(2,1)} %param.20), kind=kLoop, calls=%fused_computation.163 | loop fusion | bytes 5898240 | tf_op jit(solution)/shard_map/slice | solution.py:27
  41.6 110.5 %all-gather.3.cloned.1.call-done = bf16[1,64,64,128]{3,2,0,1:T(8,128)(2,1)} async-done(((bf16[1,1,64,128]{3,2,0,1:T(8,128)(2,1)}), bf16[1,64,64,128]{3,2,0,1:T(8,128)(2,1)}) %all-gather.3.cloned.1.call-update) | async-done | bytes 1048592 | tf_op jit(solution)/shard_map/all_gather | solution.py:93
  152.2 5.0 %reshape.308 = bf16[4096,2,64]{2,1,0:T(2,128)(2,1)} reshape(bf16[1,64,64,128]{3,2,0,1:T(8,128)(2,1)} %all-gather.3.cloned.1.call-done) | data formatting | bytes 2097152 | tf_op jit(solution)/shard_map/reshape
  157.2 2.5 fusion.89
  159.7 0.4 fusion.5
  160.1 132.0 %all-gather.5.cloned.1.call-done = bf16[1,64,64,128]{3,2,0,1:T(8,128)(2,1)} async-done(((bf16[1,1,64,128]{3,2,0,1:T(8,128)(2,1)}), bf16[1,64,64,128]{3,2,0,1:T(8,128)(2,1)}) %all-gather.5.cloned.1.call-update) | async-done | bytes 1048592 | tf_op jit(solution)/shard_map/all_gather | solution.py:96
  292.1 5.0 %reshape.309 = bf16[4096,2,64]{2,1,0:T(2,128)(2,1)} reshape(bf16[1,64,64,128]{3,2,0,1:T(8,128)(2,1)} %all-gather.5.cloned.1.call-done) | data formatting | bytes 2097152 | tf_op jit(solution)/shard_map/reshape.4
  297.1 2.3 fusion.28
  299.6 0.9 fusion.1
  300.5 1.9 fusion.87
  302.4 80.3 %all-reduce.4.cloned.1.call-done = bf16[1,1,64,1920]{3,2,1,0:T(8,128)(2,1)} async-done(((bf16[1,1,64,1920]{3,2,1,0:T(8,128)(2,1)}), bf16[1,1,64,1920]{3,2,1,0:T(8,128)(2,1)}) %all-reduce.4.cloned.1.call-update) | async-done | bytes 245776 | tf_op jit(solution)/shard_map/psum | solution.py:119
  382.7 1.1 fusion.44
  383.9 1.2 multiply_reduce_fusion
  385.1 1.1 add_convert_fusion
  386.3 11.0 %collective-permute-start = (bf16[1,1,64,1920]{3,2,1,0:T(8,128)(2,1)S(1)}, bf16[1,1,64,1920]{3,2,1,0:T(8,128)(2,1)S(1)}, u32[]{:S(2)}, u32[]{:S(2)}) collective-permute-start(bf16[1,1,64,1920]{3,2,1,0:T(8,128)(2,1)S(1)} %add_convert_fusion), channel_id=1, source_target_pairs={{0,8},{8,16},{16,24},{24,32},{32,40},{40,48},{48,56},{56,64},{64,7... | collective-permute-start | bytes 737288 | tf_op jit(solution)/shard_map/ppermute | solution.py:20
  397.2 1.9 collective-permute-start.1
  399.2 0.2 fusion.58
  399.4 0.2 fusion.55
  399.6 0.7 collective-permute-done
  400.4 8.0 %collective-permute-done.1 = bf16[1,1,64,1920]{3,2,1,0:T(8,128)(2,1)S(1)} collective-permute-done((bf16[1,1,64,1920]{3,2,1,0:T(8,128)(2,1)S(1)}, bf16[1,1,64,1920]{3,2,1,0:T(8,128)(2,1)S(1)}, u32[]{:S(2)}, u32[]{:S(2)}) %collective-permute-start.1) | collective-permute-done | bytes 245792 | tf_op jit(solution)/shard_map/ppermute | solution.py:21
  408.4 0.2 fusion.39
  408.6 0.2 fusion.49
  408.8 0.2 fusion.61
  409.1 0.2 convolution_add_fusion.20
  409.3 0.2 convolution_add_fusion.18
  409.5 0.2 convolution_add_fusion.17
  409.8 0.2 fusion.22
  410.0 0.2 fusion.24
  410.4 1.2 fusion.48
  411.6 1.2 fusion.47
  412.9 0.2 fusion.21
  413.1 1.2 fusion.20
  414.3 0.2 convolution_add_fusion.13
  414.5 0.2 convolution_add_fusion.12
  414.8 0.2 fusion.19
  415.3 22.5 %all_gather.15 = bf16[1,2,128,384]{2,1,0,3:T(2,128)(2,1)S(1)} all-gather(bf16[1,2,128,48]{2,1,0,3:T(2,128)(2,1)S(1)} %copy.252), channel_id=1, replica_groups=mesh['seq'=64,'mp'=8] {'mp'}, dimensions={3}, use_global_device_ids=true | all-gather | bytes 221184 | tf_op jit(solution)/shard_map/all_gather | solution.py:126
  438.0 0.2 fusion.71
  438.2 7.8 %collective-permute-start.2 = (bf16[1,1,128,384]{3,2,1,0:T(8,128)(2,1)S(1)}, bf16[1,1,128,384]{3,2,1,0:T(8,128)(2,1)S(1)}, u32[]{:S(2)}, u32[]{:S(2)}) collective-permute-start(bf16[1,1,128,384]{3,2,1,0:T(8,128)(2,1)S(1)} %get-tuple-element.37), channel_id=1, source_target_pairs={{0,8},{8,16},{16,24},{24,32},{32,40},{40,48},{48,56},{56,64},{64,7... | collective-permute-start | bytes 294920 | tf_op jit(solution)/shard_map/ppermute | solution.py:20
  446.0 1.9 collective-permute-start.3
  447.9 0.2 fusion.68
  448.2 7.4 %collective-permute-done.3 = bf16[1,1,128,384]{3,2,1,0:T(8,128)(2,1)S(1)} collective-permute-done((bf16[1,1,128,384]{3,2,1,0:T(8,128)(2,1)S(1)}, bf16[1,1,128,384]{3,2,1,0:T(8,128)(2,1)S(1)}, u32[]{:S(2)}, u32[]{:S(2)}) %collective-permute-start.3) | collective-permute-done | bytes 98336 | tf_op jit(solution)/shard_map/ppermute | solution.py:21
  455.7 0.2 fusion.65
  455.9 0.2 fusion.73
  456.1 0.2 convolution_add_fusion.10
  456.4 0.2 convolution_add_fusion.8
  456.6 0.2 convolution_add_fusion.7
  456.8 0.2 fusion.16
  457.0 0.2 fusion.18
  457.5 0.2 fusion.63
  457.7 0.2 fusion.62
  457.9 0.2 fusion.15
  458.2 0.2 fusion.14
  458.4 0.2 convolution_add_fusion.3
  458.6 0.2 convolution_add_fusion.2
  458.8 0.2 fusion.13
  459.6 0.4 reshape.310
  460.0 8.2 %all_to_all.15 = bf16[8,2,3072]{2,1,0:T(2,128)(2,1)S(1)} all-to-all(bf16[8,2,3072]{2,1,0:T(2,128)(2,1)S(1)} %reshape.310), channel_id=1, replica_groups=mesh['seq'=64,'mp'=8] {'mp'}, dimensions={0} | all-to-all | bytes 196608 | tf_op jit(solution)/shard_map/all_to_all | solution.py:132
  468.3 0.2 reshape.311
  468.7 0.2 reshape.290
  468.9 0.9 fusion.9
  (103 shorter events, 2.2 us)
Async XLA Ops:
  6.5 293.0 %copy-start = (bf16[128,1920]{1,0:T(8,128)(2,1)S(1)}, bf16[128,1920]{1,0:T(8,128)(2,1)}, u32[]{:S(2)}) copy-start(bf16[128,1920]{1,0:T(8,128)(2,1)} %param.17) | copy-start | bytes 1474564
  6.5 145.7 %all-gather.3.cloned.1.call-start = ((), (), s32[]{:S(2)}) async-start(), calls=%async_computation.1 | async-start | bytes 1064960 | tf_op jit(solution)/shard_map/all_gather | solution.py:93
  7.3 284.9 %all-gather.5.cloned.1.call-start = ((), (), s32[]{:S(2)}) async-start(), calls=%async_computation.2 | async-start | bytes 1064960 | tf_op jit(solution)/shard_map/all_gather | solution.py:96
  8.0 374.7 %all-reduce.4.cloned.1.call-start = ((), (), s32[]{:S(2)}) async-start(), calls=%async_computation.3 | async-start | bytes 491520 | tf_op jit(solution)/shard_map/psum | solution.py:119
  297.1 3.4 copy-start.1
  299.5 85.5 %copy-start.31 = (f32[1920]{0:T(1024)S(1)}, f32[1920]{0:T(1024)}, u32[]{:S(2)}) copy-start(f32[1920]{0:T(1024)} %param.19) | copy-start | bytes 23044
  299.6 85.5 %copy-start.32 = (f32[1920]{0:T(1024)S(1)}, f32[1920]{0:T(1024)}, u32[]{:S(2)}) copy-start(f32[1920]{0:T(1024)} %param.18) | copy-start | bytes 23044
  300.5 98.6 %copy-start.3 = (bf16[48,1,1,1920]{3,2,1,0:T(2,128)(2,1)S(1)}, bf16[48,1,1,1920]{3,2,1,0:T(2,128)(2,1)}, u32[]{:S(2)}) copy-start(bf16[48,1,1,1920]{3,2,1,0:T(2,128)(2,1)} %get-tuple-element.19) | copy-start | bytes 552964
  300.5 98.9 %copy-start.2 = (bf16[48,1,1,1920]{3,2,1,0:T(2,128)(2,1)S(1)}, bf16[48,1,1,1920]{3,2,1,0:T(2,128)(2,1)}, u32[]{:S(2)}) copy-start(bf16[48,1,1,1920]{3,2,1,0:T(2,128)(2,1)} %get-tuple-element.10) | copy-start | bytes 552964
  302.4 106.2 %copy-start.14 = (bf16[48,1,1,1920]{3,2,1,0:T(2,128)(2,1)S(1)}, bf16[48,1,1,1920]{3,2,1,0:T(2,128)(2,1)}, u32[]{:S(2)}) copy-start(bf16[48,1,1,1920]{3,2,1,0:T(2,128)(2,1)} %get-tuple-element.17) | copy-start | bytes 552964
  383.8 25.0 %copy-start.13 = (bf16[48,1,1,1920]{3,2,1,0:T(2,128)(2,1)S(1)}, bf16[48,1,1,1920]{3,2,1,0:T(2,128)(2,1)}, u32[]{:S(2)}) copy-start(bf16[48,1,1,1920]{3,2,1,0:T(2,128)(2,1)} %get-tuple-element.16) | copy-start | bytes 552964
  385.1 23.9 %copy-start.12 = (bf16[48,1,1,1920]{3,2,1,0:T(2,128)(2,1)S(1)}, bf16[48,1,1,1920]{3,2,1,0:T(2,128)(2,1)}, u32[]{:S(2)}) copy-start(bf16[48,1,1,1920]{3,2,1,0:T(2,128)(2,1)} %get-tuple-element.18) | copy-start | bytes 552964
  386.3 14.1 %collective-permute-start = (bf16[1,1,64,1920]{3,2,1,0:T(8,128)(2,1)S(1)}, bf16[1,1,64,1920]{3,2,1,0:T(8,128)(2,1)S(1)}, u32[]{:S(2)}, u32[]{:S(2)}) collective-permute-start(bf16[1,1,64,1920]{3,2,1,0:T(8,128)(2,1)S(1)} %add_convert_fusion), channel_id=1, source_target_pairs={{0,8},{8,16},{16,24},{24,32},{32,40},{40,48},{48,56},{56,64},{64,7... | collective-permute-start | bytes 737288 | tf_op jit(solution)/shard_map/ppermute | solution.py:20
  397.2 11.1 %collective-permute-start.1 = (bf16[1,1,64,1920]{3,2,1,0:T(8,128)(2,1)S(1)}, bf16[1,1,64,1920]{3,2,1,0:T(8,128)(2,1)S(1)}, u32[]{:S(2)}, u32[]{:S(2)}) collective-permute-start(bf16[1,1,64,1920]{3,2,1,0:T(8,128)(2,1)S(1)} %add_convert_fusion), channel_id=1, source_target_pairs={{8,0},{16,8},{24,16},{32,24},{40,32},{48,40},{56,48},{64,56},{72,6... | collective-permute-start | bytes 737288 | tf_op jit(solution)/shard_map/ppermute | solution.py:21
  399.2 10.1 %copy-start.9 = (bf16[48,1,1,1920]{3,2,1,0:T(2,128)(2,1)S(1)}, bf16[48,1,1,1920]{3,2,1,0:T(2,128)(2,1)}, u32[]{:S(2)}) copy-start(bf16[48,1,1,1920]{3,2,1,0:T(2,128)(2,1)} %get-tuple-element.15) | copy-start | bytes 552964
  399.4 10.1 %copy-start.11 = (bf16[48,1,1,1920]{3,2,1,0:T(2,128)(2,1)S(1)}, bf16[48,1,1,1920]{3,2,1,0:T(2,128)(2,1)}, u32[]{:S(2)}) copy-start(bf16[48,1,1,1920]{3,2,1,0:T(2,128)(2,1)} %get-tuple-element.14) | copy-start | bytes 552964
  399.6 10.1 %copy-start.8 = (bf16[48,1,1,1920]{3,2,1,0:T(2,128)(2,1)S(1)}, bf16[48,1,1,1920]{3,2,1,0:T(2,128)(2,1)}, u32[]{:S(2)}) copy-start(bf16[48,1,1,1920]{3,2,1,0:T(2,128)(2,1)} %get-tuple-element.13) | copy-start | bytes 552964
  408.6 1.4 copy-start.7
  409.1 3.8 copy-start.6
  409.5 4.8 copy-start.5
  409.8 4.8 %copy-start.10 = (bf16[48,1,1,1920]{3,2,1,0:T(2,128)(2,1)S(1)}, bf16[48,1,1,1920]{3,2,1,0:T(2,128)(2,1)}, u32[]{:S(2)}) copy-start(bf16[48,1,1,1920]{3,2,1,0:T(2,128)(2,1)} %get-tuple-element.6) | copy-start | bytes 552964
  410.2 4.6 copy-start.4
  410.4 4.8 %copy-start.34 = (f32[48]{0:T(128)S(1)}, f32[48]{0:T(128)}, u32[]{:S(2)}) copy-start(f32[48]{0:T(128)} %param.21) | copy-start | bytes 580
  412.9 25.2 %copy-start.16 = (bf16[48,1,1,384]{3,2,1,0:T(2,128)(2,1)S(1)}, bf16[48,1,1,384]{3,2,1,0:T(2,128)(2,1)}, u32[]{:S(2)}) copy-start(bf16[48,1,1,384]{3,2,1,0:T(2,128)(2,1)} %get-tuple-element.35) | copy-start | bytes 110596
  414.5 41.2 %copy-start.30 = (bf16[48,1,1,384]{3,2,1,0:T(2,128)(2,1)S(1)}, bf16[48,1,1,384]{3,2,1,0:T(2,128)(2,1)}, u32[]{:S(2)}) copy-start(bf16[48,1,1,384]{3,2,1,0:T(2,128)(2,1)} %get-tuple-element.33) | copy-start | bytes 110596
  414.5 41.4 %copy-start.29 = (bf16[48,1,1,384]{3,2,1,0:T(2,128)(2,1)S(1)}, bf16[48,1,1,384]{3,2,1,0:T(2,128)(2,1)}, u32[]{:S(2)}) copy-start(bf16[48,1,1,384]{3,2,1,0:T(2,128)(2,1)} %get-tuple-element.32) | copy-start | bytes 110596
  414.8 41.4 %copy-start.22 = (bf16[48,1,1,384]{3,2,1,0:T(2,128)(2,1)S(1)}, bf16[48,1,1,384]{3,2,1,0:T(2,128)(2,1)}, u32[]{:S(2)}) copy-start(bf16[48,1,1,384]{3,2,1,0:T(2,128)(2,1)} %get-tuple-element.34) | copy-start | bytes 110596
  414.8 41.6 %copy-start.21 = (bf16[48,1,1,384]{3,2,1,0:T(2,128)(2,1)S(1)}, bf16[48,1,1,384]{3,2,1,0:T(2,128)(2,1)}, u32[]{:S(2)}) copy-start(bf16[48,1,1,384]{3,2,1,0:T(2,128)(2,1)} %get-tuple-element.31) | copy-start | bytes 110596
  415.0 41.5 %copy-start.28 = (bf16[48,1,1,384]{3,2,1,0:T(2,128)(2,1)S(1)}, bf16[48,1,1,384]{3,2,1,0:T(2,128)(2,1)}, u32[]{:S(2)}) copy-start(bf16[48,1,1,384]{3,2,1,0:T(2,128)(2,1)} %get-tuple-element.30) | copy-start | bytes 110596
  437.8 19.0 %copy-start.20 = (bf16[48,1,1,384]{3,2,1,0:T(2,128)(2,1)S(1)}, bf16[48,1,1,384]{3,2,1,0:T(2,128)(2,1)}, u32[]{:S(2)}) copy-start(bf16[48,1,1,384]{3,2,1,0:T(2,128)(2,1)} %get-tuple-element.29) | copy-start | bytes 110596
  438.0 19.0 %copy-start.24 = (bf16[48,1,1,384]{3,2,1,0:T(2,128)(2,1)S(1)}, bf16[48,1,1,384]{3,2,1,0:T(2,128)(2,1)}, u32[]{:S(2)}) copy-start(bf16[48,1,1,384]{3,2,1,0:T(2,128)(2,1)} %get-tuple-element.21) | copy-start | bytes 110596
  438.2 9.9 %collective-permute-start.2 = (bf16[1,1,128,384]{3,2,1,0:T(8,128)(2,1)S(1)}, bf16[1,1,128,384]{3,2,1,0:T(8,128)(2,1)S(1)}, u32[]{:S(2)}, u32[]{:S(2)}) collective-permute-start(bf16[1,1,128,384]{3,2,1,0:T(8,128)(2,1)S(1)} %get-tuple-element.37), channel_id=1, source_target_pairs={{0,8},{8,16},{16,24},{24,32},{32,40},{40,48},{48,56},{56,64},{64,7... | collective-permute-start | bytes 294920 | tf_op jit(solution)/shard_map/ppermute | solution.py:20
  446.0 9.5 %collective-permute-start.3 = (bf16[1,1,128,384]{3,2,1,0:T(8,128)(2,1)S(1)}, bf16[1,1,128,384]{3,2,1,0:T(8,128)(2,1)S(1)}, u32[]{:S(2)}, u32[]{:S(2)}) collective-permute-start(bf16[1,1,128,384]{3,2,1,0:T(8,128)(2,1)S(1)} %get-tuple-element.38), channel_id=1, source_target_pairs={{8,0},{16,8},{24,16},{32,24},{40,32},{48,40},{56,48},{64,56},{72,6... | collective-permute-start | bytes 294920 | tf_op jit(solution)/shard_map/ppermute | solution.py:21
  448.1 9.4 %copy-start.27 = (bf16[48,1,1,384]{3,2,1,0:T(2,128)(2,1)S(1)}, bf16[48,1,1,384]{3,2,1,0:T(2,128)(2,1)}, u32[]{:S(2)}) copy-start(bf16[48,1,1,384]{3,2,1,0:T(2,128)(2,1)} %get-tuple-element.27) | copy-start | bytes 110596
  455.7 2.0 copy-start.26
  455.9 2.0 copy-start.23
  456.1 2.0 copy-start.19
  456.3 2.0 copy-start.18
  456.6 2.0 copy-start.25
  456.8 2.0 copy-start.17
  457.5 1.8 copy-start.35
  458.8 10.1 %copy-start.15 = (bf16[384,308]{0,1:T(8,128)(2,1)S(1)}, bf16[384,308]{0,1:T(8,128)(2,1)}, u32[]{:S(2)}) copy-start(bf16[384,308]{0,1:T(8,128)(2,1)} %param.24) | copy-start | bytes 709636
  458.8 10.1 %copy-start.33 = (f32[308]{0:T(512)S(1)}, f32[308]{0:T(512)}, u32[]{:S(2)}) copy-start(f32[308]{0:T(512)} %param.25) | copy-start | bytes 3700
Sparse Core Ops, SparseCore 0:
  10.6 141.5 all-gather.2
  155.5 136.5 all-gather.4
  300.6 82.0 all-reduce.3
where the time goes:
time: 477 us; the launch traced here: 476 us
  waiting for transfers between devices  340 us (71%)
  blocking collectives  53.1 us (11%)
  local copies, waits for them, and re-layouts  25.6 us (5%)
  starting transfers between devices  22.7 us (5%)
  matrix products  16 us (3%)
  between operations  14.1 us (3%)
    all_gather x1, waiting for transfers between devices, local(): lax.all_gather(values, 'seq', axis=1, tiled=True)  132 us
    all_gather x1, waiting for transfers between devices, local(): lax.all_gather(keys, 'seq', axis=1, tiled=True)  111 us
    psum x1, waiting for transfers between devices, local(): lax.psum(partial_value.astype(jnp.bfloat16), 'mp').astype(jnp.float32)  80.3 us
    all_gather x1, blocking collectives, local(): gathered = lax.all_gather(hidden_one, 'mp', axis=3, tiled=True)  22.5 us
    all_gather x1, blocking collectives, local(): full_resid = lax.all_gather(resid, 'mp', axis=2, tiled=True)  22.4 us
    ppermute x2, starting transfers between devices, with_halo(): before = lax.ppermute(last, axis, up)  18.7 us
    ppermute x2, waiting for transfers between devices, with_halo(): after = lax.ppermute(first, axis, down)  15.4 us
    slice x2, local copies, waits for them, and re-layouts, tap_product(): tap = weight[:, kernel_row, kernel_col, :]  12.3 us
  transfers between devices with their start and end apart: 7, of which 6 were waited for; matrix products, arithmetic and copies ran while one was open for 5% of the time, Pallas kernels for 0%

commit v1 on v0

v1 whole, which is shorter than its diff:
```python
import jax
import jax.numpy as jnp
from jax import lax
from jax.experimental import pallas as pl
from jax.experimental.pallas import tpu as pltpu
from jax.sharding import PartitionSpec as P

EPSILON = 1e-06
MESH = pl.DeviceIdType.MESH
F32 = jnp.float32
BF16 = jnp.bfloat16
ROWS = 64
COLS = 64
PEERS = 8
LAYERS = 16
CHANNELS = 48
TAPS = (1, 2, 3, 0)
CHUNK = 8


def nt(a, b):
    return lax.dot_general(a, b, (((1,), (1,)), ((), ())), preferred_element_type=F32)


def nn(a, b):
    return lax.dot_general(a, b, (((1,), (0,)), ((), ())), preferred_element_type=F32)


def shifted(field):
    row = lax.broadcasted_iota(jnp.int32, field.shape, 0) & (COLS - 1)
    lane = lax.broadcasted_iota(jnp.int32, field.shape, 1) & 127
    before = jnp.where(row == 0, 0.0, pltpu.roll(field, 1, 0))
    after = jnp.where(row == COLS - 1, 0.0, pltpu.roll(field, field.shape[0] - 1, 0))
    return jnp.where(lane < CHANNELS, before, after)


def body(
    q_ref, k_ref, v_ref, resid_ref, wo_ref, gain_ref, shift_ref, w1_ref, b1_ref, w2_ref, b2_ref, wf_ref, bf_ref,
    out_ref,
    kv, other, qb, qsend, asend, arecv, scores, part, got, normed, halo1s, halo1r, one, halo2s, halo2r, two, tiles,
    pair_s, pair_r, right_s, right_r, left_s, left_r, mp_s, mp_r, halo_s, halo_r,
):
    s = lax.axis_index("seq")
    m = lax.axis_index("mp")
    core = lax.rem(s, 2)
    y = lax.rem(lax.div(s, 2), 2)
    z = lax.div(s, 4)

    def seq_at(zz, yy, cc):
        return zz * 4 + yy * 2 + cc

    mate = seq_at(z, y, 1 - core)
    across = seq_at(z, 1 - y, core)
    diagonal = seq_at(z, 1 - y, 1 - core)
    z_up = lax.rem(s + 4, ROWS)
    z_down = lax.rem(s + ROWS - 4, ROWS)
    row_up = lax.rem(s + 1, ROWS)
    row_down = lax.rem(s + ROWS - 1, ROWS)

    barrier = pltpu.get_barrier_semaphore()
    greeted = [(mate, m), (across, m), (diagonal, m), (z_up, m), (z_down, m), (row_up, m), (row_down, m)]
    greeted += [(s, lax.rem(m + d, PEERS)) for d in range(1, PEERS)]
    for device in greeted:
        pl.semaphore_signal(barrier, inc=1, device_id=device, device_id_type=MESH)

    lane = lax.broadcasted_iota(jnp.int32, (COLS, 128), 1)
    low = lane < 64
    k = k_ref[...].astype(F32)
    v = v_ref[...].astype(F32)
    q = q_ref[...].astype(F32) * 0.125
    first = jnp.where(low, k, pltpu.roll(v, 64, 1))
    second = jnp.where(low, pltpu.roll(k, 64, 1), v)
    q_first = jnp.where(low, q, 0.0)
    q_second = jnp.where(low, pltpu.roll(q, 64, 1), 0.0)
    is_first = core == 0
    kv[s] = jnp.where(is_first, first, second).astype(BF16)
    other[...] = jnp.where(is_first, second, first).astype(BF16)
    qb[core] = jnp.where(is_first, q_first, q_second).astype(BF16)
    qsend[...] = jnp.where(is_first, q_second, q_first).astype(BF16)

    pl.semaphore_wait(barrier, len(greeted))

    def send(src, dst, ssem, rsem, device):
        return pltpu.make_async_remote_copy(
            src_ref=src, dst_ref=dst, send_sem=ssem, recv_sem=rsem, device_id=device, device_id_type=MESH
        )

    def piece(layer, p):
        yy = y if p < 2 else 1 - y
        cc = core if p % 2 == 0 else 1 - core
        return seq_at(layer, yy, cc)

    def right(t, p):
        block = kv.at[piece(lax.rem(z - t + LAYERS, LAYERS), p)]
        return send(block, block, right_s.at[t, p], right_r.at[t, p], (z_up, m))

    def left(t, p):
        block = kv.at[piece(lax.rem(z + t, LAYERS), p)]
        return send(block, block, left_s.at[t, p], left_r.at[t, p], (z_down, m))

    right(0, 0).start()
    left(0, 0).start()
    pair = [
        None,
        send(other, kv.at[s], pair_s.at[1], pair_r.at[1], (mate, m)),
        send(kv.at[s], kv.at[s], pair_s.at[2], pair_r.at[2], (across, m)),
        send(other, kv.at[s], pair_s.at[3], pair_r.at[3], (diagonal, m)),
        send(qsend, qb.at[core], pair_s.at[0], pair_r.at[0], (mate, m)),
    ]
    for p in (1, 2, 3, 4):
        pair[p].start()
    for p in (1, 2, 3):
        pair[p].wait_recv()
        right(0, p).start()
        left(0, p).start()

    def ring(t, carry):
        for p in range(4):
            right(t - 1, p).wait_recv()
            right(t, p).start()
            left(t - 1, p).wait_recv()
            left(t, p).start()
        return carry

    lax.fori_loop(1, 7, ring, 0)
    for p in range(4):
        right(6, p).wait_recv()
        right(7, p).start()
    for p in range(4):
        left(6, p).wait_recv()
    pair[4].wait_recv()
    for p in range(4):
        right(7, p).wait_recv()

    queries = qb[...].reshape(2 * COLS, 128)

    def score(j, best):
        block = kv[pl.ds(j * CHUNK, CHUNK)].reshape(CHUNK * COLS, 128)
        fresh = nt(queries, block)
        scores[j] = fresh
        return jnp.maximum(best, jnp.max(fresh, axis=1, keepdims=True))

    top = lax.fori_loop(0, ROWS // CHUNK, score, jnp.full((2 * COLS, 1), -jnp.inf, F32))

    def mix(j, carry):
        total, mixed = carry
        exps = jnp.exp(scores[j] - top)
        block = kv[pl.ds(j * CHUNK, CHUNK)].reshape(CHUNK * COLS, 128)
        return total + jnp.sum(exps, axis=1, keepdims=True), mixed + nn(exps.astype(BF16), block)

    total, mixed = lax.fori_loop(
        0, ROWS // CHUNK, mix, (jnp.zeros((2 * COLS, 1), F32), jnp.zeros((2 * COLS, 128), F32))
    )
    attended = mixed / total
    placed = jnp.where(is_first, jnp.where(low, pltpu.roll(attended[:COLS], 64, 1), 0.0), jnp.where(low, 0.0, attended[:COLS]))
    placed_too = jnp.where(is_first, jnp.where(low, pltpu.roll(attended[COLS:], 64, 1), 0.0), jnp.where(low, 0.0, attended[COLS:]))
    asend[...] = jnp.where(is_first, placed_too, placed).astype(BF16)
    swap = send(asend, arecv, pair_s.at[4], pair_r.at[4], (mate, m))
    swap.start()
    mine = jnp.where(is_first, placed, placed_too).astype(BF16)
    swap.wait_recv()
    rows = (mine.astype(F32) + arecv[...].astype(F32)).astype(BF16)

    def exchange(phase, source, target):
        copies = []
        for d in range(1, PEERS):
            peer = lax.rem(m + d, PEERS)
            copies.append(send(source(peer), target, mp_s.at[phase, d], mp_r.at[phase, d], (s, peer)))
        for copy in copies:
            copy.start()
        return copies

    def arrived(copies):
        for copy in copies:
            copy.wait_recv()

    part[...] = nn(rows, wo_ref[...]).reshape(PEERS, 8, -1).astype(BF16)
    sums = exchange(0, lambda peer: part.at[peer], got.at[m])
    stream = resid_ref[...].astype(F32) + part[m].astype(F32)
    got[m] = jnp.zeros(got.shape[1:], BF16)
    arrived(sums)
    for j in range(PEERS):
        stream = stream + got[j].astype(F32)
    center = jnp.mean(stream, axis=1, keepdims=True)
    apart = stream - center
    variance = jnp.mean(apart * apart, axis=1, keepdims=True)
    normed[m] = (apart * lax.rsqrt(variance + EPSILON) * gain_ref[...] + shift_ref[...]).astype(BF16)
    norms = exchange(1, lambda peer: normed.at[m], normed.at[m])
    arrived(norms)
    tokens = normed[...].astype(F32).reshape(COLS, -1).astype(BF16)

    def first_block(i):
        return nt(tokens, w1_ref[pl.ds(i * 256, 256), :])

    crossing = first_block(2) + shifted(first_block(3))
    halo1s[0] = crossing[:, :128]
    halo1s[1] = crossing[:, 128:]
    to_up = send(halo1s.at[0], halo1r.at[0], halo_s.at[0], halo_r.at[0], (row_up, m))
    to_down = send(halo1s.at[1], halo1r.at[1], halo_s.at[1], halo_r.at[1], (row_down, m))
    to_up.start()
    to_down.start()
    inside = first_block(0) + shifted(first_block(1))
    to_up.wait_recv()
    to_down.wait_recv()
    upper = inside[:, :128] + jnp.where(s > 0, halo1r[0], 0.0)
    lower = inside[:, 128:] + jnp.where(s < ROWS - 1, halo1r[1], 0.0)
    one[m, 0] = jnp.maximum(upper + b1_ref[...], 0.0).astype(BF16)
    one[m, 1] = jnp.maximum(lower + b1_ref[...], 0.0).astype(BF16)
    ones = exchange(2, lambda peer: one.at[m], one.at[m])
    arrived(ones)
    cells = jnp.concatenate([one[j].reshape(2 * COLS, 128) for j in range(PEERS)], axis=1)

    def second_block(i):
        product = nt(cells, w2_ref[pl.ds(i * 384, 384), :])
        return product[:, :128] + shifted(product[:, 256:]), product[:, 128:256]

    down_first, down_second = second_block(2)
    up_first, up_second = second_block(3)
    halo2s[0, :, :128] = down_first[COLS:]
    halo2s[0, :, 128:] = down_second[COLS:]
    halo2s[1, :, :128] = up_first[:COLS]
    halo2s[1, :, 128:] = up_second[:COLS]
    to_up2 = send(halo2s.at[0], halo2r.at[0], halo_s.at[2], halo_r.at[2], (row_up, m))
    to_down2 = send(halo2s.at[1], halo2r.at[1], halo_s.at[3], halo_r.at[3], (row_down, m))
    to_up2.start()
    to_down2.start()
    even_first, even_second = second_block(0)
    odd_first, odd_second = second_block(1)
    halves = [
        [even_first[:COLS], even_second[:COLS]],
        [odd_first[:COLS] + up_first[COLS:], odd_second[:COLS] + up_second[COLS:]],
        [even_first[COLS:] + down_first[:COLS], even_second[COLS:] + down_second[:COLS]],
        [odd_first[COLS:], odd_second[COLS:]],
    ]
    to_up2.wait_recv()
    to_down2.wait_recv()
    for h in range(2):
        lanes = slice(h * 128, h * 128 + 128)
        halves[0][h] = halves[0][h] + jnp.where(s > 0, halo2r[0, :, lanes], 0.0)
        halves[3][h] = halves[3][h] + jnp.where(s < ROWS - 1, halo2r[1, :, lanes], 0.0)
        for r in range(4):
            block = jnp.maximum(halves[r][h] + b2_ref[...], 0.0)
            two[:, h, r] = block.reshape(PEERS, 8, 128).astype(BF16)
    tiles[m] = two[m]
    twos = exchange(3, lambda peer: two.at[peer], tiles.at[m])
    arrived(twos)
    positions = jnp.concatenate(
        [tiles[j].astype(F32).reshape(64, 128).astype(BF16) for j in range(PEERS)], axis=1
    )
    last = nn(positions, wf_ref[...])
    count = out_ref.shape[-1]
    apart_maps = [(last[:, v * 384 : v * 384 + count] + bf_ref[...]).astype(BF16) for v in range(2)]
    maps = jnp.concatenate(apart_maps, axis=0)
    place = lax.broadcasted_iota(jnp.int32, (128, 128), 0)
    source = (
        ((place >> 1) & 1) * 64
        + ((place ^ (place >> 1)) & 1) * 32
        + (place >> 5) * 8
        + ((place >> 2) & 7)
    )
    order = jnp.where(lax.broadcasted_iota(jnp.int32, (128, 128), 1) == source, 1.0, 0.0).astype(BF16)
    out_ref[...] = nn(order, maps).astype(BF16).reshape(out_ref.shape)

    for p in (1, 2, 3, 4):
        pair[p].wait_send()
    swap.wait_send()

    def sent(t, carry):
        for p in range(4):
            right(t, p).wait_send()
            left(t, p).wait_send()
        return carry

    lax.fori_loop(0, 7, sent, 0)
    for p in range(4):
        right(7, p).wait_send()
    for copy in sums + norms + ones + twos + [to_up, to_down, to_up2, to_down2]:
        copy.wait_send()


def taps_one(weight):
    width = weight.shape[-1]
    blocks = []
    for role in range(2):
        for side in range(2):
            for a in range(2):
                for b in range(2):
                    blocks.append(weight[:, TAPS[role * 2 + a], TAPS[side * 2 + b], :])
                blocks.append(jnp.zeros((32, width), weight.dtype))
    return jnp.concatenate(blocks, axis=0)


def taps_two(weight):
    by_peer = weight.reshape(CHANNELS, 4, 4, PEERS, CHANNELS)
    blank = jnp.zeros((CHANNELS, PEERS, CHANNELS), weight.dtype)
    gap = jnp.zeros((32, PEERS, 2 * CHANNELS), weight.dtype)
    columns = ((1, None), (None, 2), (), (2, 0), (3, 1), (), (None, 3), (0, None), ())
    blocks = []
    for tap in TAPS:
        for pair in columns:
            if pair:
                blocks.append(
                    jnp.concatenate([blank if t is None else by_peer[:, tap, t] for t in pair], axis=2)
                )
            else:
                blocks.append(gap)
    joined = jnp.pad(jnp.concatenate(blocks, axis=0), ((0, 0), (0, 0), (0, 32)))
    return joined.reshape(joined.shape[0], PEERS * 128)


def final_pair(weight):
    by_peer = weight.reshape(PEERS, CHANNELS, -1)
    wide = 384 - by_peer.shape[-1]
    low = jnp.pad(by_peer, ((0, 0), (0, 80), (0, wide)))
    high = jnp.pad(by_peer, ((0, 0), (48, 32), (0, wide)))
    return jnp.concatenate([low, high], axis=2).reshape(PEERS * 128, 768)


def twice(bias):
    return jnp.concatenate([bias, bias, jnp.zeros((32,), bias.dtype)])[None]


def local(
    query, keys, values, resid, out_weight, norm_gain, norm_bias,
    deconv1_weight, deconv1_bias, deconv2_weight, deconv2_bias, final_weight, final_bias,
):
    width = resid.shape[-1]
    count = final_weight.shape[-1]
    operands = (
        query.reshape(COLS, 128),
        keys.reshape(COLS, 128),
        values.reshape(COLS, 128),
        resid.reshape(8, width),
        out_weight,
        norm_gain[None],
        norm_bias[None],
        taps_one(deconv1_weight),
        twice(deconv1_bias),
        taps_two(deconv2_weight),
        twice(deconv2_bias),
        final_pair(final_weight),
        final_bias[None],
    )
    dma = pltpu.SemaphoreType.DMA
    vmem = pltpu.VMEM
    out = pl.pallas_call(
        body,
        out_shape=jax.ShapeDtypeStruct((4, 32, count), BF16),
        in_specs=[pl.BlockSpec(memory_space=pltpu.VMEM)] * len(operands),
        out_specs=pl.BlockSpec(memory_space=pltpu.VMEM),
        scratch_shapes=[
            vmem((ROWS, COLS, 128), BF16),
            vmem((COLS, 128), BF16),
            vmem((2, COLS, 128), BF16),
            vmem((COLS, 128), BF16),
            vmem((COLS, 128), BF16),
            vmem((COLS, 128), BF16),
            vmem((ROWS // CHUNK, 2 * COLS, CHUNK * COLS), F32),
            vmem((PEERS, 8, width), BF16),
            vmem((PEERS, 8, width), BF16),
            vmem((PEERS, 8, width), BF16),
            vmem((2, COLS, 128), F32),
            vmem((2, COLS, 128), F32),
            vmem((PEERS, 2, COLS, 128), BF16),
            vmem((2, COLS, 256), F32),
            vmem((2, COLS, 256), F32),
            vmem((PEERS, 2, 4, 8, 128), BF16),
            vmem((PEERS, 2, 4, 8, 128), BF16),
            dma((5,)),
            dma((5,)),
            dma((8, 4)),
            dma((8, 4)),
            dma((7, 4)),
            dma((7, 4)),
            dma((4, PEERS)),
            dma((4, PEERS)),
            dma((4,)),
            dma((4,)),
        ],
        compiler_params=pltpu.CompilerParams(
            collective_id=0, has_side_effects=True, vmem_limit_bytes=60 * 1024 * 1024
        ),
        name="head",
    )(*operands)
    return out[None]


def solution(mesh):
    placed = (
        P(None, "seq", None, "mp"),
        P(None, "seq", None, "mp"),
        P(None, "seq", None, "mp"),
        P(None, "seq", "mp", None),
        P("mp", None),
        P(),
        P(),
        P("mp", None, None, None),
        P("mp"),
        P("mp", None, None, None),
        P("mp"),
        P(),
        P(),
    )
    return jax.shard_map(
        local, mesh=mesh, in_specs=placed, out_specs=P(None, "seq", "mp", None), check_vma=False
    )
```

time: 477 us -> 109 us (0.23)
  the two profiles are of different devices: /device:TPU:113 before, /device:TPU:8 now
where the time goes in v1:
time: 109 us
  Pallas kernels  83.8 us (77%)
  local copies, waits for them, and re-layouts  21.9 us (20%)
  other arithmetic  3.11 us (3%)
    pallas_call x1, Pallas kernels, local(): pl.pallas_call(body, out_shape=jax.ShapeDtypeStruct((4, 32, count), BF16)...  83.8 us
    slice x1, local copies, waits for them, and re-layouts, taps_one(): blocks.append(weight[:, TAPS[role * 2 + a], TAPS[side * 2 + b], :])  9 us
    unnamed x65, local copies, waits for them, and re-layouts  7.27 us

profile of v1, /device:TPU:8, one launch (start us, length us, event | category | flops | bytes accessed | tf_op | source)
XLA Modules:
  0.0 109.1 jit_solution(6986184384010072426)
XLA Ops:
  0.0 1.3 %broadcast_in_dim.22.gain_ref = f32[1,1920]{1,0:T(1,128)} reshape(f32[1920]{0:T(1024)} %param.18) | data formatting | bytes 15360 | tf_op jit(solution)/shard_map/broadcast_in_dim | solution.py:335
  1.3 1.3 %broadcast_in_dim.23.shift_ref = f32[1,1920]{1,0:T(1,128)} reshape(f32[1920]{0:T(1024)} %param.19) | data formatting | bytes 15360 | tf_op jit(solution)/shard_map/broadcast_in_dim | solution.py:336
  2.6 9.0 %fusion.21 = (bf16[48,1,1,1920]{3,2,1,0:T(2,128)(2,1)S(1)}, bf16[48,1,1,1920]{3,2,1,0:T(2,128)(2,1)S(1)}, bf16[48,1,1,1920]{3,2,1,0:T(2,128)(2,1)S(1)}, bf16[48,...) fusion(bf16[48,4,4,1920]{3,2,1,0:T(4,128)(2,1)} %param.20), kind=kLoop, calls=%fused_computation.102 | loop fusion | bytes 5898240 | tf_op jit(solution)/shard_map/slice | solution.py:288
  11.8 0.0 copy-start.4
  11.9 0.0 copy-start.5
  11.9 0.0 copy-start.1
  12.3 0.0 copy-start
  12.4 0.1 copy-done.4
  12.5 0.0 copy-done.5
  12.5 0.8 fusion.20
  13.3 0.9 copy-done
  14.2 0.0 copy-done.1
  14.2 1.4 %reshape.28 = bf16[48,4,4,8,48]{4,3,2,1,0:T(8,128)(2,1)S(1)} reshape(bf16[48,4,4,384]{3,2,1,0:T(4,128)(2,1)S(1)} %copy-done.1) | data formatting | bytes 1179648 | tf_op jit(solution)/shard_map/reshape | solution.py:294
  15.6 0.4 slice_bitcast_fusion
  16.1 0.1 constant_dynamic-update-slice_fusion.42
  16.2 0.1 constant_dynamic-update-slice_fusion.40
  16.3 0.1 constant_dynamic-update-slice_fusion.39
  16.4 0.1 constant_dynamic-update-slice_fusion.37
  16.7 0.1 constant_dynamic-update-slice_fusion.33
  16.8 0.1 constant_dynamic-update-slice_fusion.31
  16.9 0.1 constant_dynamic-update-slice_fusion.30
  17.1 0.1 constant_dynamic-update-slice_fusion.28
  17.3 0.1 constant_dynamic-update-slice_fusion.24
  17.4 0.1 constant_dynamic-update-slice_fusion.22
  17.5 0.1 constant_dynamic-update-slice_fusion.21
  17.7 0.1 constant_dynamic-update-slice_fusion.19
  17.9 0.1 constant_dynamic-update-slice_fusion.15
  18.0 0.1 constant_dynamic-update-slice_fusion.13
  18.1 0.1 constant_dynamic-update-slice_fusion.12
  18.3 0.1 constant_dynamic-update-slice_fusion.10
  18.4 0.7 pad.28
  19.1 0.0 copy-start.2
  19.1 0.0 copy-start.3
  19.1 2.5 %copy.163 = bf16[192,8,8,128]{3,1,2,0:T(8,128)(2,1)} copy(bf16[192,8,8,128]{3,2,1,0:T(8,128)(2,1)S(1)} %bitcast.143) | data formatting | bytes 6291456
  21.6 0.0 copy-done.2
  21.6 0.2 copy.80
  21.9 1.4 %fusion.2 = bf16[8,128,768]{2,1,0:T(8,128)(2,1)} fusion(bf16[8,48,308]{2,1,0:T(8,128)(2,1)S(1)} %bitcast.146), kind=kLoop, calls=%fused_computation.5 | loop fusion | flops 6291456 | bytes 1809408 | tf_op jit(solution)/shard_map/concatenate | solution.py:316
  23.2 0.0 copy-done.3
  23.2 0.6 broadcast_in_dim.27.bf_ref
  23.8 83.8 %head.1 = bf16[4,32,308]{2,1,0:T(8,128)(2,1)} custom-call(bf16[64,128]{1,0:T(8,128)(2,1)} %bitcast.149, bf16[64,128]{1,0:T(8,128)(2,1)} %bitcast.150, bf16[64,128]{1,0:T(8,128)(2,1)} %bitcast.151, bf16[8,1920]{1,0:T(8,128)(2,1)} %bitcast.148, bf16[128,1920]{1,0:T(8,128)(2,1)} %wo_ref.1, f32[1,1920]{1,0:T(1,128)} %broadcast_in_dim.22.gain_ref, ...), custom_call_target="tpu_custom_call" | custom-call | tf_op jit(solution)/shard_map/head/pallas_call | solution.py:346
  107.6 1.5 %copy.223 = bf16[1,4,32,308]{3,2,1,0:T(8,128)(2,1)} copy(bf16[1,4,32,308]{3,2,1,0:T(8,128)(2,1)} %bitcast.147) | data formatting | bytes 157696
  (45 shorter events, 1.0 us)
Async XLA Ops:
  11.8 0.7 copy-start.4
  11.9 0.7 copy-start.5
  11.9 2.4 %copy-start.1 = (bf16[48,4,4,384]{3,2,1,0:T(4,128)(2,1)S(1)}, bf16[48,4,4,384]{3,2,1,0:T(4,128)(2,1)}, u32[]{:S(2)}) copy-start(bf16[48,4,4,384]{3,2,1,0:T(4,128)(2,1)} %param.22) | copy-start | bytes 1769476
  12.3 1.9 %copy-start = (bf16[1024,1920]{1,0:T(8,128)(2,1)}, bf16[1024,1920]{1,0:T(8,128)(2,1)S(1)}, u32[]{:S(2)}) copy-start(bf16[1024,1920]{1,0:T(8,128)(2,1)S(1)} %constant_dynamic-update-slice_fusion.w1_ref) | copy-start | bytes 11796484
  19.1 2.5 %copy-start.2 = (bf16[384,308]{0,1:T(8,128)(2,1)S(1)}, bf16[384,308]{0,1:T(8,128)(2,1)}, u32[]{:S(2)}) copy-start(bf16[384,308]{0,1:T(8,128)(2,1)} %param.24) | copy-start | bytes 709636
  19.1 4.1 %copy-start.3 = (f32[308]{0:T(512)S(1)}, f32[308]{0:T(512)}, u32[]{:S(2)}) copy-start(f32[308]{0:T(512)} %param.25) | copy-start | bytes 3700

commit v2 on v1

--- a/solution.py
+++ b/solution.py
@@ -14,8 +14,8 @@
 PEERS = 8
 LAYERS = 16
 CHANNELS = 48
-TAPS = (1, 2, 3, 0)
-CHUNK = 8
+NONE = -4096
+COLUMN_TAPS = (((1, NONE), (NONE, 2)), ((2, 0), (3, 1)), ((NONE, 3), (0, NONE)))
 
 
 def nt(a, b):
@@ -24,6 +24,10 @@
 
 def nn(a, b):
     return lax.dot_general(a, b, (((1,), (0,)), ((), ())), preferred_element_type=F32)
+
+
+def tn(a, b):
+    return lax.dot_general(a, b, (((0,), (0,)), ((), ())), preferred_element_type=F32)
 
 
 def shifted(field):
@@ -35,10 +39,10 @@
 
 
 def body(
-    q_ref, k_ref, v_ref, resid_ref, wo_ref, gain_ref, shift_ref, w1_ref, b1_ref, w2_ref, b2_ref, wf_ref, bf_ref,
+    q_ref, k_ref, v_ref, resid_ref, wo_ref, gain_ref, shift_ref, w1_hbm, b1_ref, w2_hbm, b2_ref, wf_hbm, bf_ref,
     out_ref,
-    kv, other, qb, qsend, asend, arecv, scores, part, got, normed, halo1s, halo1r, one, halo2s, halo2r, two, tiles,
-    pair_s, pair_r, right_s, right_r, left_s, left_r, mp_s, mp_r, halo_s, halo_r,
+    w1_four, w1_raw, w1, w2_four, w2_raw, w2, wf_raw, wf_low, wf_high, low_spread, high_spread, kv, other, qb, qsend, asend, arecv, part, got, normed, halo1s, halo1r, one, halo2s, halo2r, two, tiles,
+    pair_s, pair_r, right_s, right_r, left_s, left_r, mp_s, mp_r, halo_s, halo_r, load_s,
 ):
     s = lax.axis_index("seq")
     m = lax.axis_index("mp")
@@ -56,6 +60,13 @@
     z_down = lax.rem(s + ROWS - 4, ROWS)
     row_up = lax.rem(s + 1, ROWS)
     row_down = lax.rem(s + ROWS - 1, ROWS)
+
+    loads = [
+        pltpu.make_async_copy(hbm, raw, load_s.at[i])
+        for i, (hbm, raw) in enumerate(((w1_hbm, w1_four), (w2_hbm, w2_four), (wf_hbm, wf_raw)))
+    ]
+    for copy in loads:
+        copy.start()
 
     barrier = pltpu.get_barrier_semaphore()
     greeted = [(mate, m), (across, m), (diagonal, m), (z_up, m), (z_down, m), (row_up, m), (row_down, m)]
@@ -113,44 +124,117 @@
         pair[p].wait_recv()
         right(0, p).start()
         left(0, p).start()
-
-    def ring(t, carry):
+    pair[4].wait_recv()
+
+    def attend(state, layers):
+        top, total, mixed = state
+        block = jnp.concatenate([kv[pl.ds(layer * 4, 4)].reshape(4 * COLS, 128) for layer in layers], axis=0)
+        fresh = nt(qb[...].reshape(2 * COLS, 128), block)
+        best = jnp.maximum(top, jnp.max(fresh, axis=1, keepdims=True))
+        fade = jnp.exp(top - best)
+        exps = jnp.exp(fresh - best)
+        return (
+            best,
+            total * fade + jnp.sum(exps, axis=1, keepdims=True),
+            mixed * fade + nn(exps.astype(BF16), block),
+        )
+
+    def arrange_one(i):
+        row_tap = lax.rem(lax.div(i, 4) * 2 + lax.rem(i, 2) + 1, 4)
+        side = lax.rem(lax.div(i, 2), 2) * 2
+        col_tap = jnp.where(group, lax.rem(side + 2, 4), lax.rem(side + 1, 4))
+        source = channel * 16 + row_tap * 4 + col_tap
+        w1[pl.ds(pl.multiple_of(i * 128, 128), 128), :] = nn(pick(source, 768), w1_raw[...]).astype(BF16)
+
+    def arrange_two(i, n):
+        row_tap = lax.rem(i + 1, 4)
+        for b, spread in ((0, low_spread), (1, high_spread)):
+            first_tap, second_tap = [
+                jnp.where(n == 0, COLUMN_TAPS[0][g][b], jnp.where(n == 1, COLUMN_TAPS[1][g][b], COLUMN_TAPS[2][g][b]))
+                for g in range(2)
+            ]
+            col_tap = jnp.where(group, second_tap, first_tap)
+            rows = nn(pick(channel * 16 + row_tap * 4 + col_tap, 768), w2_raw[...]).astype(BF16)
+            placed = nn(rows, spread[...])
+            full = placed if b == 0 else full + placed
+        w2[pl.ds(pl.multiple_of(i * 384 + n * 128, 128), 128), :] = full.astype(BF16)
+
+    line = lax.broadcasted_iota(jnp.int32, (128, 768), 0)
+    group = line >= CHANNELS
+    channel = jnp.where(group, line - CHANNELS, line)
+    kept = line < 2 * CHANNELS
+
+    def pick(source, width):
+        wanted = jnp.where(kept, source, -1)
+        return jnp.where(lax.broadcasted_iota(jnp.int32, (128, width), 1) == wanted, 1.0, 0.0).astype(BF16)
+
+    wide = lax.broadcasted_iota(jnp.int32, (PEERS * CHANNELS, PEERS * 128), 1)
+    narrow = lax.broadcasted_iota(jnp.int32, (PEERS * CHANNELS, PEERS * 128), 0)
+    within = wide & 127
+    home = (wide >> 7) * CHANNELS + within
+    low_spread[...] = jnp.where((narrow == home) & (within < CHANNELS), 1.0, 0.0).astype(BF16)
+    high_spread[...] = jnp.where(
+        (narrow == home - CHANNELS) & (within >= CHANNELS) & (within < 2 * CHANNELS), 1.0, 0.0
+    ).astype(BF16)
+    bias1 = twice(b1_ref[...])
+    bias2 = twice(b2_ref[...])
+    for copy in loads:
+        copy.wait()
+
+    def flatten(four, raw, first, last):
+        def rows_of(e, carry):
+            rows = pl.ds(pl.multiple_of(e * 32, 32), 32)
+            raw[rows, :] = four[pl.ds(e * 2, 2)].astype(F32).reshape(32, raw.shape[1]).astype(BF16)
+            return carry
+
+        lax.fori_loop(first, last, rows_of, 0)
+
+    def arrange_part(first):
+        def chunk(i, carry):
+            arrange_two(lax.div(i, 3), lax.rem(i, 3))
+            return carry
+
+        lax.fori_loop(first, first + 4, chunk, 0)
+
+    start = (
+        jnp.full((2 * COLS, 1), -jnp.inf, F32),
+        jnp.zeros((2 * COLS, 1), F32),
+        jnp.zeros((2 * COLS, 128), F32),
+    )
+    state = attend(start, [z])
+
+    def ring(t, state):
         for p in range(4):
             right(t - 1, p).wait_recv()
             right(t, p).start()
             left(t - 1, p).wait_recv()
             left(t, p).start()
-        return carry
-
-    lax.fori_loop(1, 7, ring, 0)
+        return attend(state, [lax.rem(z - t + LAYERS, LAYERS), lax.rem(z + t, LAYERS)])
+
+    def ring_flatten(t, state):
+        state = ring(t, state)
+        flatten(w1_four, w1_raw, (t - 1) * 8, t * 8)
+        return state
+
+    def ring_arrange(t, state):
+        state = ring(t, state)
+        arrange_one((t - 4) * 2)
+        arrange_one((t - 4) * 2 + 1)
+        return state
+
+    state = lax.fori_loop(1, 4, ring_flatten, state)
+    state = lax.fori_loop(4, 7, ring_arrange, state)
     for p in range(4):
         right(6, p).wait_recv()
         right(7, p).start()
     for p in range(4):
         left(6, p).wait_recv()
-    pair[4].wait_recv()
+    state = attend(state, [lax.rem(z + 9, LAYERS), lax.rem(z + 7, LAYERS)])
+    arrange_one(6)
+    arrange_one(7)
     for p in range(4):
         right(7, p).wait_recv()
-
-    queries = qb[...].reshape(2 * COLS, 128)
-
-    def score(j, best):
-        block = kv[pl.ds(j * CHUNK, CHUNK)].reshape(CHUNK * COLS, 128)
-        fresh = nt(queries, block)
-        scores[j] = fresh
-        return jnp.maximum(best, jnp.max(fresh, axis=1, keepdims=True))
-
-    top = lax.fori_loop(0, ROWS // CHUNK, score, jnp.full((2 * COLS, 1), -jnp.inf, F32))
-
-    def mix(j, carry):
-        total, mixed = carry
-        exps = jnp.exp(scores[j] - top)
-        block = kv[pl.ds(j * CHUNK, CHUNK)].reshape(CHUNK * COLS, 128)
-        return total + jnp.sum(exps, axis=1, keepdims=True), mixed + nn(exps.astype(BF16), block)
-
-    total, mixed = lax.fori_loop(
-        0, ROWS // CHUNK, mix, (jnp.zeros((2 * COLS, 1), F32), jnp.zeros((2 * COLS, 128), F32))
-    )
+    top, total, mixed = attend(state, [lax.rem(z + 8, LAYERS)])
     attended = mixed / total
     placed = jnp.where(is_first, jnp.where(low, pltpu.roll(attended[:COLS], 64, 1), 0.0), jnp.where(low, 0.0, attended[:COLS]))
     placed_too = jnp.where(is_first, jnp.where(low, pltpu.roll(attended[COLS:], 64, 1), 0.0), jnp.where(low, 0.0, attended[COLS:]))
@@ -178,19 +262,22 @@
     sums = exchange(0, lambda peer: part.at[peer], got.at[m])
     stream = resid_ref[...].astype(F32) + part[m].astype(F32)
     got[m] = jnp.zeros(got.shape[1:], BF16)
+    flatten(w2_four, w2_raw, 0, CHANNELS // 2)
+    arrange_part(0)
     arrived(sums)
     for j in range(PEERS):
         stream = stream + got[j].astype(F32)
     center = jnp.mean(stream, axis=1, keepdims=True)
     apart = stream - center
     variance = jnp.mean(apart * apart, axis=1, keepdims=True)
-    normed[m] = (apart * lax.rsqrt(variance + EPSILON) * gain_ref[...] + shift_ref[...]).astype(BF16)
+    normed[m] = (apart * lax.rsqrt(variance + EPSILON) * gain_ref[...][None] + shift_ref[...][None]).astype(BF16)
     norms = exchange(1, lambda peer: normed.at[m], normed.at[m])
+    arrange_part(4)
     arrived(norms)
     tokens = normed[...].astype(F32).reshape(COLS, -1).astype(BF16)
 
     def first_block(i):
-        return nt(tokens, w1_ref[pl.ds(i * 256, 256), :])
+        return nt(tokens, w1[pl.ds(i * 256, 256), :])
 
     crossing = first_block(2) + shifted(first_block(3))
     halo1s[0] = crossing[:, :128]
@@ -204,14 +291,17 @@
     to_down.wait_recv()
     upper = inside[:, :128] + jnp.where(s > 0, halo1r[0], 0.0)
     lower = inside[:, 128:] + jnp.where(s < ROWS - 1, halo1r[1], 0.0)
-    one[m, 0] = jnp.maximum(upper + b1_ref[...], 0.0).astype(BF16)
-    one[m, 1] = jnp.maximum(lower + b1_ref[...], 0.0).astype(BF16)
+    one[m, 0] = jnp.maximum(upper + bias1, 0.0).astype(BF16)
+    one[m, 1] = jnp.maximum(lower + bias1, 0.0).astype(BF16)
     ones = exchange(2, lambda peer: one.at[m], one.at[m])
+    arrange_part(8)
+    wf_low[...] = nn(wf_raw[...], low_spread[...]).astype(BF16)
+    wf_high[...] = nn(wf_raw[...], high_spread[...]).astype(BF16)
     arrived(ones)
     cells = jnp.concatenate([one[j].reshape(2 * COLS, 128) for j in range(PEERS)], axis=1)
 
     def second_block(i):
-        product = nt(cells, w2_ref[pl.ds(i * 384, 384), :])
+        product = nt(cells, w2[pl.ds(i * 384, 384), :])
         return product[:, :128] + shifted(product[:, 256:]), product[:, 128:256]
 
     down_first, down_second = second_block(2)
@@ -239,7 +329,7 @@
         halves[0][h] = halves[0][h] + jnp.where(s > 0, halo2r[0, :, lanes], 0.0)
         halves[3][h] = halves[3][h] + jnp.where(s < ROWS - 1, halo2r[1, :, lanes], 0.0)
         for r in range(4):
-            block = jnp.maximum(halves[r][h] + b2_ref[...], 0.0)
+            block = jnp.maximum(halves[r][h] + bias2, 0.0)
             two[:, h, r] = block.reshape(PEERS, 8, 128).astype(BF16)
     tiles[m] = two[m]
     twos = exchange(3, lambda peer: two.at[peer], tiles.at[m])
@@ -247,9 +337,7 @@
     positions = jnp.concatenate(
         [tiles[j].astype(F32).reshape(64, 128).astype(BF16) for j in range(PEERS)], axis=1
     )
-    last = nn(positions, wf_ref[...])
-    count = out_ref.shape[-1]
-    apart_maps = [(last[:, v * 384 : v * 384 + count] + bf_ref[...]).astype(BF16) for v in range(2)]
+    apart_maps = [(nt(positions, weight[...]) + bf_ref[...][None]).astype(BF16) for weight in (wf_low, wf_high)]
     maps = jnp.concatenate(apart_maps, axis=0)
     place = lax.broadcasted_iota(jnp.int32, (128, 128), 0)
     source = (
@@ -278,46 +366,11 @@
         copy.wait_send()
 
 
-def taps_one(weight):
-    width = weight.shape[-1]
-    blocks = []
-    for role in range(2):
-        for side in range(2):
-            for a in range(2):
-                for b in range(2):
-                    blocks.append(weight[:, TAPS[role * 2 + a], TAPS[side * 2 + b], :])
-                blocks.append(jnp.zeros((32, width), weight.dtype))
-    return jnp.concatenate(blocks, axis=0)
-
-
-def taps_two(weight):
-    by_peer = weight.reshape(CHANNELS, 4, 4, PEERS, CHANNELS)
-    blank = jnp.zeros((CHANNELS, PEERS, CHANNELS), weight.dtype)
-    gap = jnp.zeros((32, PEERS, 2 * CHANNELS), weight.dtype)
-    columns = ((1, None), (None, 2), (), (2, 0), (3, 1), (), (None, 3), (0, None), ())
-    blocks = []
-    for tap in TAPS:
-        for pair in columns:
-            if pair:
-                blocks.append(
-                    jnp.concatenate([blank if t is None else by_peer[:, tap, t] for t in pair], axis=2)
-                )
-            else:
-                blocks.append(gap)
-    joined = jnp.pad(jnp.concatenate(blocks, axis=0), ((0, 0), (0, 0), (0, 32)))
-    return joined.reshape(joined.shape[0], PEERS * 128)
-
-
-def final_pair(weight):
-    by_peer = weight.reshape(PEERS, CHANNELS, -1)
-    wide = 384 - by_peer.shape[-1]
-    low = jnp.pad(by_peer, ((0, 0), (0, 80), (0, wide)))
-    high = jnp.pad(by_peer, ((0, 0), (48, 32), (0, wide)))
-    return jnp.concatenate([low, high], axis=2).reshape(PEERS * 128, 768)
-
-
 def twice(bias):
-    return jnp.concatenate([bias, bias, jnp.zeros((32,), bias.dtype)])[None]
+    lane = lax.broadcasted_iota(jnp.int32, (CHANNELS, 128), 1)
+    home = jnp.where(lane < CHANNELS, lane, lane - CHANNELS)
+    spread = jnp.where(lax.broadcasted_iota(jnp.int32, (CHANNELS, 128), 0) == home, 1.0, 0.0)
+    return jnp.dot(jnp.broadcast_to(bias[None], (8, CHANNELS)), spread, precision=lax.Precision.HIGHEST)[:1]
 
 
 def local(
@@ -332,30 +385,42 @@
         values.reshape(COLS, 128),
         resid.reshape(8, width),
         out_weight,
-        norm_gain[None],
-        norm_bias[None],
-        taps_one(deconv1_weight),
-        twice(deconv1_bias),
-        taps_two(deconv2_weight),
-        twice(deconv2_bias),
-        final_pair(final_weight),
-        final_bias[None],
+        norm_gain,
+        norm_bias,
+        deconv1_weight,
+        deconv1_bias,
+        deconv2_weight,
+        deconv2_bias,
+        final_weight.T,
+        final_bias,
     )
     dma = pltpu.SemaphoreType.DMA
     vmem = pltpu.VMEM
     out = pl.pallas_call(
         body,
         out_shape=jax.ShapeDtypeStruct((4, 32, count), BF16),
-        in_specs=[pl.BlockSpec(memory_space=pltpu.VMEM)] * len(operands),
+        in_specs=[
+            pl.BlockSpec(memory_space=pl.ANY if i in (7, 9, 11) else pltpu.VMEM) for i in range(len(operands))
+        ],
         out_specs=pl.BlockSpec(memory_space=pltpu.VMEM),
         scratch_shapes=[
+            vmem((CHANNELS, 4, 4, width), BF16),
+            vmem((768, width), BF16),
+            vmem((1024, width), BF16),
+            vmem((CHANNELS, 4, 4, 384), BF16),
+            vmem((768, 384), BF16),
+            vmem((1536, 1024), BF16),
+            vmem((count, 384), BF16),
+            vmem((count, 1024), BF16),
+            vmem((count, 1024), BF16),
+            vmem((384, 1024), BF16),
+            vmem((384, 1024), BF16),
             vmem((ROWS, COLS, 128), BF16),
             vmem((COLS, 128), BF16),
             vmem((2, COLS, 128), BF16),
             vmem((COLS, 128), BF16),
             vmem((COLS, 128), BF16),
             vmem((COLS, 128), BF16),
-            vmem((ROWS // CHUNK, 2 * COLS, CHUNK * COLS), F32),
             vmem((PEERS, 8, width), BF16),
             vmem((PEERS, 8, width), BF16),
             vmem((PEERS, 8, width), BF16),
@@ -376,6 +441,7 @@
             dma((4, PEERS)),
             dma((4,)),
             dma((4,)),
+            dma((3,)),
         ],
         compiler_params=pltpu.CompilerParams(
             collective_id=0, has_side_effects=True, vmem_limit_bytes=60 * 1024 * 1024

time: 109 us -> 80 us (0.73)
  local copies, waits for them, and re-layouts: 21.9 us -> 1.54 us
  Pallas kernels: 83.8 us -> 78.3 us
  other arithmetic: 3.11 us -> 0 us
    slice x1 -> x0, local copies, waits for them, and re-layouts: 9 us -> none  [taps_one(): blocks.append(weight[:, TAPS[role * 2 + a], TAPS[side * 2 + b], :])]
    unnamed x65 -> x1, local copies, waits for them, and re-layouts: 7.27 us -> 1.54 us
    pallas_call x1, Pallas kernels: 83.8 us -> 78.3 us  [local(): pl.pallas_call(body, out_shape=jax.ShapeDtypeStruct((4, 32, count), BF16)...]
    broadcast_in_dim x3 -> x0, local copies, waits for them, and re-layouts: 3.17 us -> none  [the longest x1 1.3 us: local(): norm_gain[None]]
    reshape x1 -> x0, local copies, waits for them, and re-layouts: 1.39 us -> none  [taps_two(): by_peer = weight.reshape(CHANNELS, 4, 4, PEERS, CHANNELS)]
    concatenate x1 -> x0, other arithmetic: 1.35 us -> none  [final_pair(): return jnp.concatenate([low, high], axis=2).reshape(PEERS * 128, 768)]
where the time goes in v2:
time: 80 us; the launch traced here: 79.8 us
  Pallas kernels  78.3 us (98%)
  local copies, waits for them, and re-layouts  1.54 us (2%)
    pallas_call x1, Pallas kernels, local(): pl.pallas_call(body, out_shape=jax.ShapeDtypeStruct((4, 32, count), BF16)...  78.3 us

profile of v2, /device:TPU:8, one launch (start us, length us, event | category | flops | bytes accessed | tf_op | source)
XLA Modules:
  0.0 79.8 jit_solution(9275812105867069167)
XLA Ops:
  0.0 78.3 %head.1 = bf16[4,32,308]{2,1,0:T(8,128)(2,1)} custom-call(bf16[64,128]{1,0:T(8,128)(2,1)} %bitcast.9, bf16[64,128]{1,0:T(8,128)(2,1)} %bitcast.10, bf16[64,128]{1,0:T(8,128)(2,1)} %bitcast.11, bf16[8,1920]{1,0:T(8,128)(2,1)} %bitcast.8, bf16[128,1920]{1,0:T(8,128)(2,1)} %wo_ref.1, f32[1920]{0:T(1024)} %gain_ref.1, f32[1920]{0:T(1024)} %shift_ref.1, ...), custom_call_target="tpu_custom_call" | custom-call | tf_op jit(solution)/shard_map/head/pallas_call | solution.py:399
  78.3 1.5 %copy.15 = bf16[1,4,32,308]{3,2,1,0:T(8,128)(2,1)} copy(bf16[1,4,32,308]{3,2,1,0:T(8,128)(2,1)} %bitcast.6) | data formatting | bytes 157696

commit v3 on v2

--- a/solution.py
+++ b/solution.py
@@ -14,8 +14,8 @@
 PEERS = 8
 LAYERS = 16
 CHANNELS = 48
-NONE = -4096
-COLUMN_TAPS = (((1, NONE), (NONE, 2)), ((2, 0), (3, 1)), ((NONE, 3), (0, NONE)))
+TAPS = (1, 2, 3, 0)
+COLUMN_TAPS = (((1, None), (None, 2)), ((2, 0), (3, 1)), ((None, 3), (0, None)))
 
 
 def nt(a, b):
@@ -41,7 +41,7 @@
 def body(
     q_ref, k_ref, v_ref, resid_ref, wo_ref, gain_ref, shift_ref, w1_hbm, b1_ref, w2_hbm, b2_ref, wf_hbm, bf_ref,
     out_ref,
-    w1_four, w1_raw, w1, w2_four, w2_raw, w2, wf_raw, wf_low, wf_high, low_spread, high_spread, kv, other, qb, qsend, asend, arecv, part, got, normed, halo1s, halo1r, one, halo2s, halo2r, two, tiles,
+    w1_four, w1_raw, w1, w2_four, w2_raw, w2_tap, w2_low, w2_high, w2, wf_raw, wf_low, wf_high, low_spread, high_spread, kv, other, qb, qsend, asend, arecv, part, got, normed, halo1s, halo1r, one, halo2s, halo2r, two, tiles,
     pair_s, pair_r, right_s, right_r, left_s, left_r, mp_s, mp_r, halo_s, halo_r, load_s,
 ):
     s = lax.axis_index("seq")
@@ -142,31 +142,12 @@
     def arrange_one(i):
         row_tap = lax.rem(lax.div(i, 4) * 2 + lax.rem(i, 2) + 1, 4)
         side = lax.rem(lax.div(i, 2), 2) * 2
-        col_tap = jnp.where(group, lax.rem(side + 2, 4), lax.rem(side + 1, 4))
-        source = channel * 16 + row_tap * 4 + col_tap
-        w1[pl.ds(pl.multiple_of(i * 128, 128), 128), :] = nn(pick(source, 768), w1_raw[...]).astype(BF16)
-
-    def arrange_two(i, n):
-        row_tap = lax.rem(i + 1, 4)
-        for b, spread in ((0, low_spread), (1, high_spread)):
-            first_tap, second_tap = [
-                jnp.where(n == 0, COLUMN_TAPS[0][g][b], jnp.where(n == 1, COLUMN_TAPS[1][g][b], COLUMN_TAPS[2][g][b]))
-                for g in range(2)
-            ]
-            col_tap = jnp.where(group, second_tap, first_tap)
-            rows = nn(pick(channel * 16 + row_tap * 4 + col_tap, 768), w2_raw[...]).astype(BF16)
-            placed = nn(rows, spread[...])
-            full = placed if b == 0 else full + placed
-        w2[pl.ds(pl.multiple_of(i * 384 + n * 128, 128), 128), :] = full.astype(BF16)
-
-    line = lax.broadcasted_iota(jnp.int32, (128, 768), 0)
-    group = line >= CHANNELS
-    channel = jnp.where(group, line - CHANNELS, line)
-    kept = line < 2 * CHANNELS
-
-    def pick(source, width):
-        wanted = jnp.where(kept, source, -1)
-        return jnp.where(lax.broadcasted_iota(jnp.int32, (128, width), 1) == wanted, 1.0, 0.0).astype(BF16)
+        for b in range(2):
+            tap = row_tap * 4 + lax.rem(side + b + 1, 4)
+            rows = pl.ds(pl.multiple_of(i * 128 + b * CHANNELS, 16), CHANNELS)
+            for c in range(w1_raw.shape[0]):
+                lanes = slice(c * 128, c * 128 + 128)
+                w1[rows, lanes] = w1_raw[c, pl.ds(tap, CHANNELS, stride=16), :].astype(BF16)
 
     wide = lax.broadcasted_iota(jnp.int32, (PEERS * CHANNELS, PEERS * 128), 1)
     narrow = lax.broadcasted_iota(jnp.int32, (PEERS * CHANNELS, PEERS * 128), 0)
@@ -184,17 +165,12 @@
     def flatten(four, raw, first, last):
         def rows_of(e, carry):
             rows = pl.ds(pl.multiple_of(e * 32, 32), 32)
-            raw[rows, :] = four[pl.ds(e * 2, 2)].astype(F32).reshape(32, raw.shape[1]).astype(BF16)
+            flat = four[pl.ds(e * 2, 2)].astype(F32).reshape(32, four.shape[-1])
+            for c in range(raw.shape[0]):
+                raw[c, rows, :] = flat[:, c * 128 : c * 128 + 128]
             return carry
 
         lax.fori_loop(first, last, rows_of, 0)
-
-    def arrange_part(first):
-        def chunk(i, carry):
-            arrange_two(lax.div(i, 3), lax.rem(i, 3))
-            return carry
-
-        lax.fori_loop(first, first + 4, chunk, 0)
 
     start = (
         jnp.full((2 * COLS, 1), -jnp.inf, F32),
@@ -202,6 +178,10 @@
         jnp.zeros((2 * COLS, 128), F32),
     )
     state = attend(start, [z])
+    for i in range(8):
+        w1[i * 128 + 2 * CHANNELS : i * 128 + 128, :] = jnp.zeros((32, w1.shape[1]), BF16)
+    for i in range(12):
+        w2[i * 128 + 2 * CHANNELS : i * 128 + 128, :] = jnp.zeros((32, w2.shape[1]), BF16)
 
     def ring(t, state):
         for p in range(4):
@@ -263,7 +243,10 @@
     stream = resid_ref[...].astype(F32) + part[m].astype(F32)
     got[m] = jnp.zeros(got.shape[1:], BF16)
     flatten(w2_four, w2_raw, 0, CHANNELS // 2)
-    arrange_part(0)
+    for tap in range(16):
+        for c in range(w2_raw.shape[0]):
+            rows = w2_raw[c, pl.ds(tap, CHANNELS, stride=16), :]
+            w2_tap[tap * CHANNELS : (tap + 1) * CHANNELS, c * 128 : c * 128 + 128] = rows.astype(BF16)
     arrived(sums)
     for j in range(PEERS):
         stream = stream + got[j].astype(F32)
@@ -272,7 +255,8 @@
     variance = jnp.mean(apart * apart, axis=1, keepdims=True)
     normed[m] = (apart * lax.rsqrt(variance + EPSILON) * gain_ref[...][None] + shift_ref[...][None]).astype(BF16)
     norms = exchange(1, lambda peer: normed.at[m], normed.at[m])
-    arrange_part(4)
+    w2_low[...] = nn(w2_tap[...], low_spread[...]).astype(BF16)
+    w2_high[...] = nn(w2_tap[...], high_spread[...]).astype(BF16)
     arrived(norms)
     tokens = normed[...].astype(F32).reshape(COLS, -1).astype(BF16)
 
@@ -294,7 +278,16 @@
     one[m, 0] = jnp.maximum(upper + bias1, 0.0).astype(BF16)
     one[m, 1] = jnp.maximum(lower + bias1, 0.0).astype(BF16)
     ones = exchange(2, lambda peer: one.at[m], one.at[m])
-    arrange_part(8)
+    for i in range(4):
+        for n in range(3):
+            base = i * 384 + n * 128
+            for g in range(2):
+                blocks = [
+                    spread[(TAPS[i] * 4 + t) * CHANNELS : (TAPS[i] * 4 + t + 1) * CHANNELS, :]
+                    for spread, t in zip((w2_low, w2_high), COLUMN_TAPS[n][g])
+                    if t is not None
+                ]
+                w2[base + g * CHANNELS : base + (g + 1) * CHANNELS, :] = sum(blocks[1:], blocks[0])
     wf_low[...] = nn(wf_raw[...], low_spread[...]).astype(BF16)
     wf_high[...] = nn(wf_raw[...], high_spread[...]).astype(BF16)
     arrived(ones)
@@ -405,10 +398,13 @@
         out_specs=pl.BlockSpec(memory_space=pltpu.VMEM),
         scratch_shapes=[
             vmem((CHANNELS, 4, 4, width), BF16),
-            vmem((768, width), BF16),
+            vmem((width // 128, 768, 128), F32),
             vmem((1024, width), BF16),
             vmem((CHANNELS, 4, 4, 384), BF16),
+            vmem((3, 768, 128), F32),
             vmem((768, 384), BF16),
+            vmem((768, 1024), BF16),
+            vmem((768, 1024), BF16),
             vmem((1536, 1024), BF16),
             vmem((count, 384), BF16),
             vmem((count, 1024), BF16),

time: 80 us -> 79.9 us (level)
  no operation moved by 1% of the time
where the time goes in v3:
time: 79.9 us; the launch traced here: 79.7 us
  Pallas kernels  78.2 us (98%)
  local copies, waits for them, and re-layouts  1.54 us (2%)
    pallas_call x1, Pallas kernels, local(): pl.pallas_call(body, out_shape=jax.ShapeDtypeStruct((4, 32, count), BF16)...  78.2 us

profile of v3, /device:TPU:8, one launch (start us, length us, event | category | flops | bytes accessed | tf_op | source)
XLA Modules:
  0.0 79.7 jit_solution(18356523159745668193)
XLA Ops:
  0.0 78.2 %head.1 = bf16[4,32,308]{2,1,0:T(8,128)(2,1)} custom-call(bf16[64,128]{1,0:T(8,128)(2,1)} %bitcast.9, bf16[64,128]{1,0:T(8,128)(2,1)} %bitcast.10, bf16[64,128]{1,0:T(8,128)(2,1)} %bitcast.11, bf16[8,1920]{1,0:T(8,128)(2,1)} %bitcast.8, bf16[128,1920]{1,0:T(8,128)(2,1)} %wo_ref.1, f32[1920]{0:T(1024)} %gain_ref.1, f32[1920]{0:T(1024)} %shift_ref.1, ...), custom_call_target="tpu_custom_call" | custom-call | tf_op jit(solution)/shard_map/head/pallas_call | solution.py:392
  78.2 1.5 %copy.15 = bf16[1,4,32,308]{3,2,1,0:T(8,128)(2,1)} copy(bf16[1,4,32,308]{3,2,1,0:T(8,128)(2,1)} %bitcast.6) | data formatting | bytes 157696

commit v4 on v3

--- a/solution.py
+++ b/solution.py
@@ -96,21 +96,14 @@
             src_ref=src, dst_ref=dst, send_sem=ssem, recv_sem=rsem, device_id=device, device_id_type=MESH
         )
 
-    def piece(layer, p):
-        yy = y if p < 2 else 1 - y
-        cc = core if p % 2 == 0 else 1 - core
-        return seq_at(layer, yy, cc)
-
-    def right(t, p):
-        block = kv.at[piece(lax.rem(z - t + LAYERS, LAYERS), p)]
-        return send(block, block, right_s.at[t, p], right_r.at[t, p], (z_up, m))
-
-    def left(t, p):
-        block = kv.at[piece(lax.rem(z + t, LAYERS), p)]
-        return send(block, block, left_s.at[t, p], left_r.at[t, p], (z_down, m))
-
-    right(0, 0).start()
-    left(0, 0).start()
+    def right(t):
+        block = kv.at[pl.ds(lax.rem(z - t + LAYERS, LAYERS) * 4, 4)]
+        return send(block, block, right_s.at[t], right_r.at[t], (z_up, m))
+
+    def left(t):
+        block = kv.at[pl.ds(lax.rem(z + t, LAYERS) * 4, 4)]
+        return send(block, block, left_s.at[t], left_r.at[t], (z_down, m))
+
     pair = [
         None,
         send(other, kv.at[s], pair_s.at[1], pair_r.at[1], (mate, m)),
@@ -118,12 +111,12 @@
         send(other, kv.at[s], pair_s.at[3], pair_r.at[3], (diagonal, m)),
         send(qsend, qb.at[core], pair_s.at[0], pair_r.at[0], (mate, m)),
     ]
-    for p in (1, 2, 3, 4):
+    for p in (3, 2, 1, 4):
         pair[p].start()
     for p in (1, 2, 3):
         pair[p].wait_recv()
-        right(0, p).start()
-        left(0, p).start()
+    right(0).start()
+    left(0).start()
     pair[4].wait_recv()
 
     def attend(state, layers):
@@ -184,11 +177,10 @@
         w2[i * 128 + 2 * CHANNELS : i * 128 + 128, :] = jnp.zeros((32, w2.shape[1]), BF16)
 
     def ring(t, state):
-        for p in range(4):
-            right(t - 1, p).wait_recv()
-            right(t, p).start()
-            left(t - 1, p).wait_recv()
-            left(t, p).start()
+        right(t - 1).wait_recv()
+        right(t).start()
+        left(t - 1).wait_recv()
+        left(t).start()
         return attend(state, [lax.rem(z - t + LAYERS, LAYERS), lax.rem(z + t, LAYERS)])
 
     def ring_flatten(t, state):
@@ -204,16 +196,13 @@
 
     state = lax.fori_loop(1, 4, ring_flatten, state)
     state = lax.fori_loop(4, 7, ring_arrange, state)
-    for p in range(4):
-        right(6, p).wait_recv()
-        right(7, p).start()
-    for p in range(4):
-        left(6, p).wait_recv()
+    right(6).wait_recv()
+    right(7).start()
+    left(6).wait_recv()
     state = attend(state, [lax.rem(z + 9, LAYERS), lax.rem(z + 7, LAYERS)])
     arrange_one(6)
     arrange_one(7)
-    for p in range(4):
-        right(7, p).wait_recv()
+    right(7).wait_recv()
     top, total, mixed = attend(state, [lax.rem(z + 8, LAYERS)])
     attended = mixed / total
     placed = jnp.where(is_first, jnp.where(low, pltpu.roll(attended[:COLS], 64, 1), 0.0), jnp.where(low, 0.0, attended[:COLS]))
@@ -347,14 +336,12 @@
     swap.wait_send()
 
     def sent(t, carry):
-        for p in range(4):
-            right(t, p).wait_send()
-            left(t, p).wait_send()
+        right(t).wait_send()
+        left(t).wait_send()
         return carry
 
     lax.fori_loop(0, 7, sent, 0)
-    for p in range(4):
-        right(7, p).wait_send()
+    right(7).wait_send()
     for copy in sums + norms + ones + twos + [to_up, to_down, to_up2, to_down2]:
         copy.wait_send()
 
@@ -429,10 +416,10 @@
             vmem((PEERS, 2, 4, 8, 128), BF16),
             dma((5,)),
             dma((5,)),
-            dma((8, 4)),
-            dma((8, 4)),
-            dma((7, 4)),
-            dma((7, 4)),
+            dma((8,)),
+            dma((8,)),
+            dma((7,)),
+            dma((7,)),
             dma((4, PEERS)),
             dma((4, PEERS)),
             dma((4,)),

time: 79.9 us -> 83 us (1.039)
  Pallas kernels: 78.2 us -> 81.3 us
    pallas_call x1, Pallas kernels: 78.2 us -> 81.3 us  [local(): pl.pallas_call(body, out_shape=jax.ShapeDtypeStruct((4, 32, count), BF16)...]
where the time goes in v4:
time: 83 us; the launch traced here: 82.8 us
  Pallas kernels  81.3 us (98%)
  local copies, waits for them, and re-layouts  1.54 us (2%)
    pallas_call x1, Pallas kernels, local(): pl.pallas_call(body, out_shape=jax.ShapeDtypeStruct((4, 32, count), BF16)...  81.3 us

profile of v4, /device:TPU:8, one launch (start us, length us, event | category | flops | bytes accessed | tf_op | source)
XLA Modules:
  0.0 82.8 jit_solution(6380124230638815662)
XLA Ops:
  0.0 81.3 %head.1 = bf16[4,32,308]{2,1,0:T(8,128)(2,1)} custom-call(bf16[64,128]{1,0:T(8,128)(2,1)} %bitcast.9, bf16[64,128]{1,0:T(8,128)(2,1)} %bitcast.10, bf16[64,128]{1,0:T(8,128)(2,1)} %bitcast.11, bf16[8,1920]{1,0:T(8,128)(2,1)} %bitcast.8, bf16[128,1920]{1,0:T(8,128)(2,1)} %wo_ref.1, f32[1920]{0:T(1024)} %gain_ref.1, f32[1920]{0:T(1024)} %shift_ref.1, ...), custom_call_target="tpu_custom_call" | custom-call | tf_op jit(solution)/shard_map/head/pallas_call | solution.py:379
  81.3 1.5 %copy.15 = bf16[1,4,32,308]{3,2,1,0:T(8,128)(2,1)} copy(bf16[1,4,32,308]{3,2,1,0:T(8,128)(2,1)} %bitcast.6) | data formatting | bytes 157696

commit v5 on v3

--- a/solution.py
+++ b/solution.py
@@ -89,6 +89,14 @@
     qb[core] = jnp.where(is_first, q_first, q_second).astype(BF16)
     qsend[...] = jnp.where(is_first, q_second, q_first).astype(BF16)
 
+    wide = lax.broadcasted_iota(jnp.int32, (PEERS * CHANNELS, PEERS * 128), 1)
+    narrow = lax.broadcasted_iota(jnp.int32, (PEERS * CHANNELS, PEERS * 128), 0)
+    within = wide & 127
+    home = (wide >> 7) * CHANNELS + within
+    low_spread[...] = jnp.where((narrow == home) & (within < CHANNELS), 1.0, 0.0).astype(BF16)
+    high_spread[...] = jnp.where(
+        (narrow == home - CHANNELS) & (within >= CHANNELS) & (within < 2 * CHANNELS), 1.0, 0.0
+    ).astype(BF16)
     pl.semaphore_wait(barrier, len(greeted))
 
     def send(src, dst, ssem, rsem, device):
@@ -118,7 +126,7 @@
         send(other, kv.at[s], pair_s.at[3], pair_r.at[3], (diagonal, m)),
         send(qsend, qb.at[core], pair_s.at[0], pair_r.at[0], (mate, m)),
     ]
-    for p in (1, 2, 3, 4):
+    for p in (2, 1, 4, 3):
         pair[p].start()
     for p in (1, 2, 3):
         pair[p].wait_recv()
@@ -149,16 +157,6 @@
                 lanes = slice(c * 128, c * 128 + 128)
                 w1[rows, lanes] = w1_raw[c, pl.ds(tap, CHANNELS, stride=16), :].astype(BF16)
 
-    wide = lax.broadcasted_iota(jnp.int32, (PEERS * CHANNELS, PEERS * 128), 1)
-    narrow = lax.broadcasted_iota(jnp.int32, (PEERS * CHANNELS, PEERS * 128), 0)
-    within = wide & 127
-    home = (wide >> 7) * CHANNELS + within
-    low_spread[...] = jnp.where((narrow == home) & (within < CHANNELS), 1.0, 0.0).astype(BF16)
-    high_spread[...] = jnp.where(
-        (narrow == home - CHANNELS) & (within >= CHANNELS) & (within < 2 * CHANNELS), 1.0, 0.0
-    ).astype(BF16)
-    bias1 = twice(b1_ref[...])
-    bias2 = twice(b2_ref[...])
     for copy in loads:
         copy.wait()
 
@@ -178,10 +176,6 @@
         jnp.zeros((2 * COLS, 128), F32),
     )
     state = attend(start, [z])
-    for i in range(8):
-        w1[i * 128 + 2 * CHANNELS : i * 128 + 128, :] = jnp.zeros((32, w1.shape[1]), BF16)
-    for i in range(12):
-        w2[i * 128 + 2 * CHANNELS : i * 128 + 128, :] = jnp.zeros((32, w2.shape[1]), BF16)
 
     def ring(t, state):
         for p in range(4):
@@ -210,6 +204,12 @@
     for p in range(4):
         left(6, p).wait_recv()
     state = attend(state, [lax.rem(z + 9, LAYERS), lax.rem(z + 7, LAYERS)])
+    bias1 = twice(b1_ref[...])
+    bias2 = twice(b2_ref[...])
+    for i in range(8):
+        w1[i * 128 + 2 * CHANNELS : i * 128 + 128, :] = jnp.zeros((32, w1.shape[1]), BF16)
+    for i in range(12):
+        w2[i * 128 + 2 * CHANNELS : i * 128 + 128, :] = jnp.zeros((32, w2.shape[1]), BF16)
     arrange_one(6)
     arrange_one(7)
     for p in range(4):

time: 79.9 us -> 80.1 us (level)
  no operation moved by 1% of the time
where the time goes in v5:
time: 80.1 us; the launch traced here: 80 us
  Pallas kernels  78.4 us (98%)
  local copies, waits for them, and re-layouts  1.54 us (2%)
    pallas_call x1, Pallas kernels, local(): pl.pallas_call(body, out_shape=jax.ShapeDtypeStruct((4, 32, count), BF16)...  78.4 us

profile of v5, /device:TPU:8, one launch (start us, length us, event | category | flops | bytes accessed | tf_op | source)
XLA Modules:
  0.0 80.0 jit_solution(5778390129632369339)
XLA Ops:
  0.0 78.4 %head.1 = bf16[4,32,308]{2,1,0:T(8,128)(2,1)} custom-call(bf16[64,128]{1,0:T(8,128)(2,1)} %bitcast.9, bf16[64,128]{1,0:T(8,128)(2,1)} %bitcast.10, bf16[64,128]{1,0:T(8,128)(2,1)} %bitcast.11, bf16[8,1920]{1,0:T(8,128)(2,1)} %bitcast.8, bf16[128,1920]{1,0:T(8,128)(2,1)} %wo_ref.1, f32[1920]{0:T(1024)} %gain_ref.1, f32[1920]{0:T(1024)} %shift_ref.1, ...), custom_call_target="tpu_custom_call" | custom-call | tf_op jit(solution)/shard_map/head/pallas_call | solution.py:392
  78.4 1.5 %copy.15 = bf16[1,4,32,308]{3,2,1,0:T(8,128)(2,1)} copy(bf16[1,4,32,308]{3,2,1,0:T(8,128)(2,1)} %bitcast.6) | data formatting | bytes 157696
